TPU v7x, 256 devices: a whole 4x4x8 slice. The times are simulated.
256 devices in a mesh: dp: 8 (over z), expert: 32 (over x, y, core).
Axes of the slice: x: 4, y: 4, z: 8, core: 2. Of those that a mesh axis runs over, the one named last changes fastest.
Arguments:
- tokens: bfloat16 [256, 212, 1024], P(('dp', 'expert')), may hold values from -6 to 6
- expert_ids: int32 [256, 212, 1], P(('dp', 'expert')), may hold values from 0 to 31; in each aligned block of 212 rows (0 to 211, 212 to 423, ..., all dimensions but the last counted through in order) at most 9 rows name the same one
- caption_lengths: int32 [256], P(('dp', 'expert')), may hold values from 1 to 16, as said below
- layer_norm_gain: float32 [1024], replicated, may hold values from 0.5 to 1.5
- router: float32 [1024, 32], replicated, may hold values from -0.1875 to 0.1875
- w_up: bfloat16 [32, 1024, 4096], P('expert', None, 'dp'), may hold values from -0.1875 to 0.1875
- w_down: bfloat16 [32, 4096, 1024], P('expert', 'dp'), may hold values from -0.09375 to 0.09375
- logit_scale: float32 [1], replicated, may hold values from 5 to 20
- logit_bias: float32 [1], replicated, may hold values from -4 to -1.5
Outputs:
- loss: float32 [1], replicated
- grad_tokens: bfloat16 [256, 212, 1024], P(('dp', 'expert'))
- grad_up: float32 [32, 1024, 4096], P('expert', None, 'dp')
- grad_down: float32 [32, 4096, 1024], P('expert', 'dp')
- grad_router: float32 [1024, 32], replicated
- layer_gain_gradient: float32 [1024], replicated
Inputs may be any that keep to these rules, and one draw needn't show every extreme that they name: `expert_ids`: among the rows of one device (aligned blocks of 212 rows, devices ordered by dp then expert) no expert is named more than 9 times, a bound that some block reaches. `caption_lengths`: some caption has all 16 tokens.
All inputs are finite; a program needn't handle non-finite values.
Results may differ from a plain program's by a relative error of at most 0.009.
Values may be sent and summed in bfloat16 or wider, within the bound.
No kernel may reach another device: no remote copies, remote signals or barrier semaphores. Data moves between devices by JAX's collectives and lax.ppermute only.
A program may use at most 128 MiB of HBM per device.

v0:
```python
import jax
import jax.numpy as jnp
from jax import lax
from jax.sharding import PartitionSpec as P

D = 1024
PATCH = 196
CAPLEN = 16
SEQ = 212
eps = 1e-06
loss_scale = 1024.0


def gelu_slope(pre):
    return (
        0.5 * (1.0 + lax.erf(pre * 0.7071067811865476))
        + pre * jnp.exp(-0.5 * pre * pre) * 0.3989422804014327
    )


def deliver(buffer, experts, slots):
    width = buffer.shape[-1]
    sent = lax.all_to_all(
        buffer.reshape(experts, 1, slots, width), "expert", split_axis=0, concat_axis=1, tiled=True
    )
    shaped = sent.reshape(sent.shape[0], 1, sent.shape[1], slots, width)
    whole = lax.all_gather(shaped, "dp", axis=1, tiled=True)
    return whole.reshape(whole.shape[0], -1, width)


def give_back(partial_value, n_dp, n_expert, slots):
    local = partial_value.shape[0]
    width = partial_value.shape[-1]
    summed = lax.psum_scatter(
        partial_value.reshape(local, n_dp, n_expert * slots, width).astype(jnp.bfloat16),
        "dp",
        scatter_dimension=1,
        tiled=True,
    )
    rounded = summed.reshape(local, n_expert, slots, width)
    returned = lax.all_to_all(rounded, "expert", split_axis=1, concat_axis=0, tiled=True)
    return returned.reshape(-1, width)


def body(
    tokens,
    expert_ids,
    caption_lengths,
    layer_norm_gain,
    router,
    w_up,
    w_down,
    logit_scale,
    logit_bias,
):
    n_dp = lax.axis_size("dp")
    n_expert = lax.axis_size("expert")
    pair_dev = tokens.shape[0]
    rows = pair_dev * SEQ
    experts = router.shape[1]
    slots = rows * 4 // (3 * experts) + 1
    pairs_all = pair_dev * n_dp * n_expert
    input_rows = tokens.reshape(rows, D).astype(jnp.float32)
    input_mean = jnp.mean(input_rows, axis=1, keepdims=True)
    var_x = jnp.mean((input_rows - input_mean) ** 2, axis=1, keepdims=True)
    inverse_deviation = 1.0 / jnp.sqrt(var_x + eps)
    centered_scaled_input = (input_rows - input_mean) * inverse_deviation
    normalized_input = (centered_scaled_input * layer_norm_gain).astype(jnp.bfloat16)
    ids = expert_ids.reshape(rows)
    onehot = (ids[:, None] == jnp.arange(experts, dtype=jnp.int32)[None, :]).astype(jnp.int32)
    slot = jnp.sum((jnp.cumsum(onehot, axis=0) - 1) * onehot, axis=1)
    dest = ids * slots + slot
    onehot_f = onehot.astype(jnp.float32)
    buffer = jnp.zeros((experts * slots, D), jnp.bfloat16).at[dest].set(normalized_input)
    gathered = deliver(buffer, experts, slots)
    pre = jnp.einsum("erd,edf->erf", gathered, w_up, preferred_element_type=jnp.float32)
    act = jax.nn.gelu(pre, approximate=False).astype(jnp.bfloat16)
    partial_value = jnp.einsum("erf,efd->erd", act, w_down, preferred_element_type=jnp.float32)
    moe = give_back(partial_value, n_dp, n_expert, slots)[dest].astype(jnp.float32)
    xnf = normalized_input.astype(jnp.float32)
    router_logits = jnp.dot(xnf, router, precision=lax.Precision.HIGHEST)
    gate = jax.nn.sigmoid(jnp.sum(router_logits * onehot_f, axis=1))
    y = (input_rows + gate[:, None] * moe).reshape(pair_dev, SEQ, D)
    img = jnp.mean(y[:, :PATCH], axis=1)
    lengths = caption_lengths.astype(jnp.float32)
    mask = (jnp.arange(CAPLEN, dtype=jnp.int32)[None, :] < caption_lengths[:, None]).astype(
        jnp.float32
    )
    txt = jnp.sum(y[:, PATCH:] * mask[:, :, None], axis=1) / lengths[:, None]
    ru = jnp.sqrt(jnp.mean(img * img, axis=1, keepdims=True) + eps)
    rv = jnp.sqrt(jnp.mean(txt * txt, axis=1, keepdims=True) + eps)
    u = img / ru
    v = txt / rv
    scale = logit_scale[0]
    first = lax.axis_index(("dp", "expert")) * pair_dev
    mine = first + jnp.arange(pair_dev, dtype=jnp.int32)
    every = jnp.arange(pairs_all, dtype=jnp.int32)
    own_sign = jnp.where(mine[:, None] == every[None, :], 1.0, -1.0)
    v_all = lax.all_gather(v, ("dp", "expert"), axis=0, tiled=True)
    logits = scale * jnp.dot(u, v_all.T, precision=lax.Precision.HIGHEST) / D + logit_bias[0]
    loss_term = -jnp.sum(jax.nn.log_sigmoid(own_sign * logits)) / pairs_all
    coef = -(loss_scale / pairs_all) * own_sign * jax.nn.sigmoid(-own_sign * logits)
    du = scale / D * jnp.dot(coef, v_all, precision=lax.Precision.HIGHEST)
    dv_terms = scale / D * jnp.dot(coef.T, u, precision=lax.Precision.HIGHEST)
    dv = lax.psum_scatter(dv_terms, ("dp", "expert"), scatter_dimension=0, tiled=True)
    dimg = (du - u * jnp.mean(du * u, axis=1, keepdims=True)) / ru
    dtxt = (dv - v * jnp.mean(dv * v, axis=1, keepdims=True)) / rv
    dy_img = jnp.broadcast_to(dimg[:, None, :] / PATCH, (pair_dev, PATCH, D))
    dy_txt = (dtxt / lengths[:, None])[:, None, :] * mask[:, :, None]
    dy = jnp.concatenate([dy_img, dy_txt], axis=1).reshape(rows, D)
    dmoe = (gate[:, None] * dy).astype(jnp.bfloat16)
    dgl = jnp.sum(dy * moe, axis=1) * gate * (1.0 - gate)
    router_part = jnp.dot(xnf.T, onehot_f * dgl[:, None], precision=lax.Precision.HIGHEST)
    grad_buffer = jnp.zeros((experts * slots, D), jnp.bfloat16).at[dest].set(dmoe)
    gathered_grads = deliver(grad_buffer, experts, slots)
    dact = jnp.einsum("erd,efd->erf", gathered_grads, w_down, preferred_element_type=jnp.float32)
    dpre = (dact * gelu_slope(pre)).astype(jnp.bfloat16)
    grad_down = jnp.einsum("erf,erd->efd", act, gathered_grads, preferred_element_type=jnp.float32)
    grad_up = jnp.einsum("erd,erf->edf", gathered, dpre, preferred_element_type=jnp.float32)
    back_partial = jnp.einsum("erf,edf->erd", dpre, w_up, preferred_element_type=jnp.float32)
    dxe = give_back(back_partial, n_dp, n_expert, slots)[dest].astype(jnp.float32)
    router_rows = jnp.dot(onehot_f, router.T, precision=lax.Precision.HIGHEST)
    gradient_normalized_input = dxe + dgl[:, None] * router_rows
    gain_partial_term = jnp.sum(gradient_normalized_input * centered_scaled_input, axis=0)
    scaled_output_gradient = gradient_normalized_input * layer_norm_gain
    normed_input_gradient = (
        scaled_output_gradient
        - jnp.mean(scaled_output_gradient, axis=1, keepdims=True)
        - centered_scaled_input
        * jnp.mean(scaled_output_gradient * centered_scaled_input, axis=1, keepdims=True)
    ) * inverse_deviation
    grad_tokens = (dy + normed_input_gradient).astype(jnp.bfloat16).reshape(pair_dev, SEQ, D)
    loss, grad_router, layer_gain_gradient = lax.psum(
        (loss_term, router_part, gain_partial_term), ("dp", "expert")
    )
    return (loss.reshape(1), grad_tokens, grad_up, grad_down, grad_router, layer_gain_gradient)


def solution(mesh):
    return jax.shard_map(
        body,
        mesh=mesh,
        in_specs=(
            P(("dp", "expert"), None, None),
            P(("dp", "expert"), None, None),
            P(("dp", "expert")),
            P(),
            P(),
            P("expert", None, "dp"),
            P("expert", "dp", None),
            P(),
            P(),
        ),
        out_specs=(
            P(),
            P(("dp", "expert"), None, None),
            P("expert", None, "dp"),
            P("expert", "dp", None),
            P(),
            P(),
        ),
        check_vma=False,
    )
```

profile of v0, /device:TPU:8, one launch (start us, length us, event | category | flops | bytes accessed | tf_op | source)
XLA Modules:
  0.0 1022.8 jit_solution(2046483523152713916)
XLA Ops:
  12.8 2.3 scatter_custom_fusion
  15.4 22.9 %all_to_all.16 = bf16[32,1,9,1024]{3,2,1,0:T(8,128)(2,1)S(1)} all-to-all(bf16[32,1,9,1024]{3,2,1,0:T(8,128)(2,1)S(1)} %bitcast.149), channel_id=1, replica_groups=mesh['dp'=8,'expert'=32] {'expert'}, dimensions={0} | all-to-all | bytes 1179648 | tf_op jit(solution)/shard_map/all_to_all | solution.py:23
  39.7 60.3 %all-gather.7.cloned.1.call-done = bf16[256,1,9,1024]{3,0,2,1:T(8,128)(2,1)} async-done(((bf16[32,1,9,1024]{3,0,2,1:T(8,128)(2,1)}), bf16[256,1,9,1024]{3,0,2,1:T(8,128)(2,1)}) %all-gather.7.cloned.1.call-update) | async-done | bytes 4718608 | tf_op jit(solution)/shard_map/all_gather | solution.py:27
  100.0 8.7 copy.22
  108.7 9.8 reshape.491
  118.6 14.9 %fusion.2 = (bf16[2304,512]{1,0:T(8,128)(2,1)S(1)}, f32[2304,512]{1,0:T(8,128)}) fusion(bf16[2304,1024]{1,0:T(8,128)(2,1)} %reshape.491, bf16[1,1024,512]{2,1,0:T(8,128)(2,1)S(1)} %copy-done), kind=kOutput, calls=%fused_computation.9 | convolution fusion | flops 2492596224 | bytes 12845056 | tf_op jit(solution)/shard_map/erd,edf->erf/dot_general | solution.py:76
  134.8 4.2 convert_bitcast_fusion.1
  139.8 58.3 %reduce-scatter.3.cloned.1.call-done = bf16[1,1,288,1024]{3,2,1,0:T(8,128)(2,1)} async-done(((bf16[1,8,288,1024]{3,2,1,0:T(8,128)(2,1)}), bf16[1,1,288,1024]{3,2,1,0:T(8,128)(2,1)}) %reduce-scatter.3.cloned.1.call-update) | async-done | bytes 589840 | tf_op jit(solution)/shard_map/reduce_scatter | solution.py:34
  198.1 2.2 reshape.494
  200.2 7.4 all-to-all-start.1
  208.8 14.4 %all-to-all-done.1 = bf16[1,32,9,1024]{3,2,0,1:T(8,128)(2,1)S(1)} async-done(((bf16[1,32,9,1024]{3,2,0,1:T(8,128)(2,1)}), bf16[1,32,9,1024]{3,2,0,1:T(8,128)(2,1)S(1)}, u32[]{:S(2)}, u32[]{:S(2)}) %all-to-all-start.1) | async-done | bytes 589856 | tf_op jit(solution)/shard_map/all_to_all | solution.py:41
  229.8 95.7 %all-gather.9.cloned.1.call-done = f32[262144]{0:T(1024)} async-done(((f32[1024]{0:T(1024)}), f32[262144]{0:T(1024)}) %all-gather.9.cloned.1.call-update) | async-done | bytes 1048592 | tf_op jit(solution)/shard_map/all_gather | solution.py:99
  331.5 254.7 %all-reduce.8.cloned.1.call-done = f32[256,1024]{1,0:T(8,128)} async-done(((f32[256,1024]{1,0:T(8,128)}), f32[256,1024]{1,0:T(8,128)}) %all-reduce.8.cloned.1.call-update) | async-done | bytes 1048592
  589.2 2.5 scatter_custom_fusion.1
  593.0 22.3 %all_to_all.17 = bf16[32,1,9,1024]{3,2,1,0:T(8,128)(2,1)S(1)} all-to-all(bf16[32,1,9,1024]{3,2,1,0:T(8,128)(2,1)S(1)} %bitcast.150), channel_id=1, replica_groups=mesh['dp'=8,'expert'=32] {'expert'}, dimensions={0} | all-to-all | bytes 1179648 | tf_op jit(solution)/shard_map/all_to_all | solution.py:23
  616.6 57.0 %all-gather.11.cloned.1.call-done = bf16[256,1,9,1024]{3,0,2,1:T(8,128)(2,1)} async-done(((bf16[32,1,9,1024]{3,0,2,1:T(8,128)(2,1)}), bf16[256,1,9,1024]{3,0,2,1:T(8,128)(2,1)}) %all-gather.11.cloned.1.call-update) | async-done | bytes 4718608 | tf_op jit(solution)/shard_map/all_gather | solution.py:27
  673.6 8.7 copy.26
  682.3 9.9 reshape.500
  692.2 7.0 fusion.14
  700.6 4.4 convert_bitcast_fusion
  707.3 7.0 convolution_bitcast_fusion
  714.3 49.8 %reduce-scatter.5.cloned.1.call-done = bf16[1,1,288,1024]{3,2,1,0:T(8,128)(2,1)} async-done(((bf16[1,8,288,1024]{3,2,1,0:T(8,128)(2,1)}), bf16[1,1,288,1024]{3,2,1,0:T(8,128)(2,1)}) %reduce-scatter.5.cloned.1.call-update) | async-done | bytes 589840 | tf_op jit(solution)/shard_map/reduce_scatter | solution.py:34
  764.1 2.2 reshape.501
  766.3 7.5 all-to-all-start.3
  773.7 7.1 convolution_bitcast_fusion.1
  780.8 8.6 all-to-all-done.3
  789.4 1.4 reshape.502
  790.8 2.0 gather_fusion.1
  792.8 2.3 fusion.37
  796.3 75.8 %all-reduce.2 = (f32[1]{0:T(128)}, f32[1024]{0:T(1024)}) all-reduce(f32[1]{0:T(128)} %bitcast.20, f32[1024]{0:T(1024)S(1)} %get-tuple-element.6), channel_id=1, replica_groups=mesh['dp'=8,'expert'=32] {'dp','expert'}, use_global_device_ids=true, to_apply=%region_13.14 | all-reduce | flops 1025 | bytes 8200 | tf_op jit(solution)/shard_map/psum | solution.py:133
  872.1 142.3 %all-reduce.6.cloned.1.call-done = f32[1024,32]{0,1:T(8,128)} async-done(((f32[1024,32]{0,1:T(8,128)}), f32[1024,32]{0,1:T(8,128)}) %all-reduce.6.cloned.1.call-update) | async-done | bytes 131088 | tf_op jit(solution)/shard_map/psum | solution.py:133
  1014.4 1.6 copy.37
  (117 shorter events, 27.8 us)
Async XLA Ops:
  7.2 111.4 %copy-start = (bf16[1,1024,512]{2,1,0:T(8,128)(2,1)S(1)}, bf16[1,1024,512]{2,1,0:T(8,128)(2,1)}, u32[]{:S(2)}) copy-start(bf16[1,1024,512]{2,1,0:T(8,128)(2,1)} %param.14) | copy-start | bytes 3145732
  7.2 92.8 %all-gather.7.cloned.1.call-start = ((), (), s32[]{:S(2)}) async-start(), calls=%async_computation.9 | async-start | bytes 5308416 | tf_op jit(solution)/shard_map/all_gather | solution.py:27
  8.5 199.2 %copy-start.11 = (f32[212]{0:T(256)}, f32[212]{0:T(256)S(1)}, u32[]{:S(2)}) copy-start(f32[212]{0:T(256)S(1)} %broadcast_multiply_fusion.3) | copy-start | bytes 2548
  9.8 197.9 %copy-start.15 = (f32[212]{0:T(256)}, f32[212]{0:T(256)S(1)}, u32[]{:S(2)}) copy-start(f32[212]{0:T(256)S(1)} %add_rsqrt_fusion) | copy-start | bytes 2548
  12.8 127.0 %copy-start.22 = (s32[212,1]{0,1:T(1,128)}, s32[212,1]{0,1:T(1,128)S(1)}, u32[]{:S(2)}) copy-start(s32[212,1]{0,1:T(1,128)S(1)} %compare_select_fusion) | copy-start | bytes 2548
  39.4 158.6 %reduce-scatter.3.cloned.1.call-start = ((), (), s32[]{:S(2)}) async-start(), calls=%async_computation.6 | async-start | bytes 5308416 | tf_op jit(solution)/shard_map/reduce_scatter | solution.py:34
  118.6 16.3 %copy-start.25 = (bf16[1,512,1024]{2,1,0:T(8,128)(2,1)S(1)}, bf16[1,512,1024]{2,1,0:T(8,128)(2,1)}, u32[]{:S(2)}) copy-start(bf16[1,512,1024]{2,1,0:T(8,128)(2,1)} %param.15) | copy-start | bytes 3145732
  133.4 1.4 copy-start.27
  139.0 68.7 %copy-start.1 = (bf16[1,212,1024]{2,1,0:T(8,128)(2,1)S(1)}, bf16[1,212,1024]{2,1,0:T(8,128)(2,1)}, u32[]{:S(2)}) copy-start(bf16[1,212,1024]{2,1,0:T(8,128)(2,1)} %param.9) | copy-start | bytes 1302532
  139.0 68.7 %copy-start.9 = (f32[1024]{0:T(1024)S(1)}, f32[1024]{0:T(1024)}, u32[]{:S(2)}) copy-start(f32[1024]{0:T(1024)} %param.12) | copy-start | bytes 12292
  139.0 69.0 %copy-start.7 = (f32[1024,32]{0,1:T(8,128)S(1)}, f32[1024,32]{0,1:T(8,128)}, u32[]{:S(2)}) copy-start(f32[1024,32]{0,1:T(8,128)} %param.13) | copy-start | bytes 393220
  139.0 69.0 %copy-start.13 = (s32[1,212,1]{1,2,0:T(1,128)S(1)}, s32[1,212,1]{1,2,0:T(1,128)}, u32[]{:S(2)}) copy-start(s32[1,212,1]{1,2,0:T(1,128)} %param.10) | copy-start | bytes 2548
  139.8 85.0 %copy-start.23 = (f32[16]{0:T(128)}, f32[16]{0:T(128)S(1)}, u32[]{:S(2)}) copy-start(f32[16]{0:T(128)S(1)} %compare_convert_fusion) | copy-start | bytes 196
  139.8 83.7 %copy-start.17 = (s32[1024]{0:T(1024)}, s32[1024]{0:T(1024)S(1)}, u32[]{:S(2)}) copy-start(s32[1024]{0:T(1024)S(1)} %pad_clamp_fusion) | copy-start | bytes 12292
  200.2 23.0 %all-to-all-start.1 = ((bf16[1,32,9,1024]{3,2,0,1:T(8,128)(2,1)}), bf16[1,32,9,1024]{3,2,0,1:T(8,128)(2,1)S(1)}, u32[]{:S(2)}, u32[]{:S(2)}) async-start(bf16[1,32,9,1024]{3,2,0,1:T(8,128)(2,1)} %bitcast.148), calls=%async_computation.2 | async-start | bytes 2097152 | tf_op jit(solution)/shard_map/all_to_all | solution.py:41
  207.7 117.8 %all-gather.9.cloned.1.call-start = ((), (), s32[]{:S(2)}) async-start(), calls=%async_computation.10 | async-start | bytes 1052672 | tf_op jit(solution)/shard_map/all_gather | solution.py:99
  208.8 14.7 %copy-start.18 = (f32[212]{0:T(256)}, f32[212]{0:T(256)S(1)}, u32[]{:S(2)}) copy-start(f32[212]{0:T(256)S(1)} %fusion.16) | copy-start | bytes 2548
  208.8 15.8 %copy-start.20 = (f32[212]{0:T(256)}, f32[212]{0:T(256)S(1)}, u32[]{:S(2)}) copy-start(f32[212]{0:T(256)S(1)} %add_divide_fusion) | copy-start | bytes 2548
  224.6 5.2 copy-start.2
  226.8 359.4 %copy-start.8 = (f32[1024]{0:T(1024)S(1)}, f32[1024]{0:T(1024)}, u32[]{:S(2)}) copy-start(f32[1024]{0:T(1024)} %broadcast_divide_fusion) | copy-start | bytes 12292
  226.8 359.4 %all-reduce.8.cloned.1.call-start = ((), (), s32[]{:S(2)}) async-start(), calls=%async_computation.12 | async-start | bytes 2097152
  228.4 360.6 %copy-start.24 = (f32[16]{0:T(128)S(1)}, f32[16]{0:T(128)}, u32[]{:S(2)}) copy-start(f32[16]{0:T(128)} %copy-done.23) | copy-start | bytes 196
  228.4 360.7 %copy-start.21 = (f32[212]{0:T(256)S(1)}, f32[212]{0:T(256)}, u32[]{:S(2)}) copy-start(f32[212]{0:T(256)} %copy-done.20) | copy-start | bytes 2548
  329.6 344.0 %all-gather.11.cloned.1.call-start = ((), (), s32[]{:S(2)}) async-start(), calls=%async_computation.11 | async-start | bytes 5308416 | tf_op jit(solution)/shard_map/all_gather | solution.py:27
  616.5 147.6 %reduce-scatter.5.cloned.1.call-start = ((), (), s32[]{:S(2)}) async-start(), calls=%async_computation.7 | async-start | bytes 5308416 | tf_op jit(solution)/shard_map/reduce_scatter | solution.py:34
  682.3 9.9 copy-start.26
  699.2 1.4 copy-start.6
  705.1 309.3 %all-reduce.6.cloned.1.call-start = ((), (), s32[]{:S(2)}) async-start(), calls=%async_computation.8 | async-start | bytes 262144 | tf_op jit(solution)/shard_map/psum | solution.py:133
  766.3 23.1 %all-to-all-start.3 = ((bf16[1,32,9,1024]{3,2,0,1:T(8,128)(2,1)}), bf16[1,32,9,1024]{3,2,0,1:T(8,128)(2,1)}, u32[]{:S(2)}, u32[]{:S(2)}) async-start(bf16[1,32,9,1024]{3,2,0,1:T(8,128)(2,1)} %bitcast.30), calls=%async_computation.5 | async-start | bytes 2097152 | tf_op jit(solution)/shard_map/all_to_all | solution.py:41
  780.8 12.0 %copy-start.10 = (f32[1024]{0:T(1024)S(1)}, f32[1024]{0:T(1024)}, u32[]{:S(2)}) copy-start(f32[1024]{0:T(1024)} %param.12) | copy-start | bytes 12292
  780.8 12.0 %copy-start.12 = (f32[212]{0:T(256)S(1)}, f32[212]{0:T(256)}, u32[]{:S(2)}) copy-start(f32[212]{0:T(256)} %copy-done.11) | copy-start | bytes 2548
  780.8 12.0 %copy-start.16 = (f32[212]{0:T(256)S(1)}, f32[212]{0:T(256)}, u32[]{:S(2)}) copy-start(f32[212]{0:T(256)} %copy-done.15) | copy-start | bytes 2548
  (5 other events, 5.5 us)
Sparse Core Ops, SparseCore 0:
  39.6 60.3 all-gather.6
  139.2 58.8 reduce-scatter.2
  226.9 98.4 all-gather.8
  331.3 254.8 all-reduce.7
  616.6 56.8 all-gather.10
  705.2 58.8 reduce-scatter.4
  771.1 243.2 all-reduce.5
where the time goes:
time: 1020 us
  waiting for transfers between devices  741 us (73%)
  blocking collectives  121 us (12%)
  local copies, waits for them, and re-layouts  56.6 us (6%)
  matrix products  49.8 us (5%)
  between operations  19.9 us (2%)
  other arithmetic  18.6 us (2%)
  starting transfers between devices  15.8 us (2%)
    unnamed x8, waiting for transfers between devices  255 us
    psum x1, waiting for transfers between devices, body(): lax.psum((loss_term, router_part, gain_partial_term), ('dp', 'expert'))  142 us
    all_gather x2, waiting for transfers between devices, deliver(): whole = lax.all_gather(shaped, 'dp', axis=1, tiled=True)  117 us
    reduce_scatter x2, waiting for transfers between devices, give_back(): lax.psum_scatter(partial_value.reshape(local, n_dp, n_expert * slots, wid...  108 us
    all_gather x1, waiting for transfers between devices, body(): v_all = lax.all_gather(v, ('dp', 'expert'), axis=0, tiled=True)  95.7 us
    psum x1, blocking collectives, body(): lax.psum((loss_term, router_part, gain_partial_term), ('dp', 'expert'))  75.8 us
    all_to_all x2, blocking collectives, deliver(): lax.all_to_all(buffer.reshape(experts, 1, slots, width), 'expert', split_...  45.2 us
    all_to_all x2, waiting for transfers between devices, give_back(): lax.all_to_all(rounded, 'expert', split_axis=1, concat_axis=0, tiled=True)  23 us
  transfers between devices with their start and end apart: 9, of which 9 were waited for; matrix products, arithmetic and copies ran while one was open for 3% of the time, Pallas kernels for 0%

commit v1 on v0

--- a/solution.py
+++ b/solution.py
@@ -38,7 +38,10 @@
         tiled=True,
     )
     rounded = summed.reshape(local, n_expert, slots, width)
-    returned = lax.all_to_all(rounded, "expert", split_axis=1, concat_axis=0, tiled=True)
+    count = lax.axis_size("expert")
+    parts = jnp.stack(jnp.split(rounded, count, axis=1), axis=0)
+    parts = lax.all_to_all(parts, "expert", split_axis=0, concat_axis=0)
+    returned = jnp.concatenate(parts, axis=0)
     return returned.reshape(-1, width)
 
 

time: 1020 us -> 1040 us (1.020)
  local copies, waits for them, and re-layouts: 56.6 us -> 93.9 us
  waiting for transfers between devices: 741 us -> 720 us
    unnamed x57 -> x125, local copies, waits for them, and re-layouts: 4.71 us -> 42.6 us
    psum x1, waiting for transfers between devices: 142 us -> 121 us  [body(): lax.psum((loss_term, router_part, gain_partial_term), ('dp', 'expert'))]
    another operation x3 -> x7, local copies, waits for them, and re-layouts: 19.8 us -> 22.7 us
  transfers between devices with their start and end apart: 9 -> 9, of which waited for: 9 -> 9; matrix products, arithmetic and copies ran while one was open for 3% -> 4% of each run, Pallas kernels for 0% -> 0%
where the time goes in v1:
time: 1040 us
  waiting for transfers between devices  720 us (69%)
  blocking collectives  121 us (12%)
  local copies, waits for them, and re-layouts  93.9 us (9%)
  matrix products  49.8 us (5%)
  between operations  20 us (2%)
  other arithmetic  18.6 us (2%)
  starting transfers between devices  15.8 us (2%)
    unnamed x8, waiting for transfers between devices  255 us
    psum x1, waiting for transfers between devices, body(): lax.psum((loss_term, router_part, gain_partial_term), ('dp', 'expert'))  121 us
    all_gather x2, waiting for transfers between devices, deliver(): whole = lax.all_gather(shaped, 'dp', axis=1, tiled=True)  117 us
    reduce_scatter x2, waiting for transfers between devices, give_back(): lax.psum_scatter(partial_value.reshape(local, n_dp, n_expert * slots, wid...  108 us
    all_gather x1, waiting for transfers between devices, body(): v_all = lax.all_gather(v, ('dp', 'expert'), axis=0, tiled=True)  95.7 us
    psum x1, blocking collectives, body(): lax.psum((loss_term, router_part, gain_partial_term), ('dp', 'expert'))  76 us
    all_to_all x2, blocking collectives, deliver(): lax.all_to_all(buffer.reshape(experts, 1, slots, width), 'expert', split_...  45.2 us
    unnamed x125, local copies, waits for them, and re-layouts  42.6 us
  transfers between devices with their start and end apart: 9, of which 9 were waited for; matrix products, arithmetic and copies ran while one was open for 4% of the time, Pallas kernels for 0%

profile of v1, /device:TPU:8, one launch (start us, length us, event | category | flops | bytes accessed | tf_op | source)
XLA Modules:
  0.0 1039.6 jit_solution(15475779433750570390)
XLA Ops:
  12.8 2.3 scatter_custom_fusion
  15.4 22.9 %all_to_all.28 = bf16[32,1,9,1024]{3,2,1,0:T(8,128)(2,1)S(1)} all-to-all(bf16[32,1,9,1024]{3,2,1,0:T(8,128)(2,1)S(1)} %bitcast.398), channel_id=1, replica_groups=mesh['dp'=8,'expert'=32] {'expert'}, dimensions={0} | all-to-all | bytes 1179648 | tf_op jit(solution)/shard_map/all_to_all | solution.py:23
  39.7 60.3 %all-gather.7.cloned.1.call-done = bf16[256,1,9,1024]{3,0,2,1:T(8,128)(2,1)} async-done(((bf16[32,1,9,1024]{3,0,2,1:T(8,128)(2,1)}), bf16[256,1,9,1024]{3,0,2,1:T(8,128)(2,1)}) %all-gather.7.cloned.1.call-update) | async-done | bytes 4718608 | tf_op jit(solution)/shard_map/all_gather | solution.py:27
  100.0 8.7 copy.22
  108.7 9.8 reshape.477
  118.6 14.9 %fusion.2 = (bf16[2304,512]{1,0:T(8,128)(2,1)S(1)}, f32[2304,512]{1,0:T(8,128)}) fusion(bf16[2304,1024]{1,0:T(8,128)(2,1)} %reshape.477, bf16[1,1024,512]{2,1,0:T(8,128)(2,1)S(1)} %copy-done), kind=kOutput, calls=%fused_computation.9 | convolution fusion | flops 2492596224 | bytes 12845056 | tf_op jit(solution)/shard_map/erd,edf->erf/dot_general | solution.py:79
  133.4 1.4 copy-done.30
  134.8 4.2 convert_bitcast_fusion.1
  139.8 58.3 %reduce-scatter.3.cloned.1.call-done = bf16[1,1,288,1024]{3,2,1,0:T(8,128)(2,1)} async-done(((bf16[1,8,288,1024]{3,2,1,0:T(8,128)(2,1)}), bf16[1,1,288,1024]{3,2,1,0:T(8,128)(2,1)}) %reduce-scatter.3.cloned.1.call-update) | async-done | bytes 589840 | tf_op jit(solution)/shard_map/reduce_scatter | solution.py:34
  219.1 7.4 all-to-all-start.1
  227.7 14.4 %all-to-all-done.1 = bf16[32,1,1,9,1024]{4,3,2,1,0:T(8,128)(2,1)S(1)} async-done(((bf16[32,1,1,9,1024]{4,3,2,1,0:T(8,128)(2,1)}), bf16[32,1,1,9,1024]{4,3,2,1,0:T(8,128)(2,1)S(1)}, u32[]{:S(2)}, u32[]{:S(2)}) %all-to-all-start.1) | async-done | bytes 589856 | tf_op jit(solution)/shard_map/all_to_all | solution.py:43
  248.7 95.7 %all-gather.9.cloned.1.call-done = f32[262144]{0:T(1024)} async-done(((f32[1024]{0:T(1024)}), f32[262144]{0:T(1024)}) %all-gather.9.cloned.1.call-update) | async-done | bytes 1048592 | tf_op jit(solution)/shard_map/all_gather | solution.py:102
  350.4 254.7 %all-reduce.8.cloned.1.call-done = f32[256,1024]{1,0:T(8,128)} async-done(((f32[256,1024]{1,0:T(8,128)}), f32[256,1024]{1,0:T(8,128)}) %all-reduce.8.cloned.1.call-update) | async-done | bytes 1048592
  608.1 2.5 scatter_custom_fusion.1
  611.9 22.3 %all_to_all.29 = bf16[32,1,9,1024]{3,2,1,0:T(8,128)(2,1)S(1)} all-to-all(bf16[32,1,9,1024]{3,2,1,0:T(8,128)(2,1)S(1)} %bitcast.399), channel_id=1, replica_groups=mesh['dp'=8,'expert'=32] {'expert'}, dimensions={0} | all-to-all | bytes 1179648 | tf_op jit(solution)/shard_map/all_to_all | solution.py:23
  635.5 57.0 %all-gather.11.cloned.1.call-done = bf16[256,1,9,1024]{3,0,2,1:T(8,128)(2,1)} async-done(((bf16[32,1,9,1024]{3,0,2,1:T(8,128)(2,1)}), bf16[256,1,9,1024]{3,0,2,1:T(8,128)(2,1)}) %all-gather.11.cloned.1.call-update) | async-done | bytes 4718608 | tf_op jit(solution)/shard_map/all_gather | solution.py:27
  692.5 8.7 copy.25
  701.2 9.9 reshape.485
  711.1 7.0 fusion.14
  718.1 1.4 copy-done.6
  719.5 4.4 convert_bitcast_fusion
  726.2 7.0 convolution_bitcast_fusion
  733.2 49.8 %reduce-scatter.5.cloned.1.call-done = bf16[1,1,288,1024]{3,2,1,0:T(8,128)(2,1)} async-done(((bf16[1,8,288,1024]{3,2,1,0:T(8,128)(2,1)}), bf16[1,1,288,1024]{3,2,1,0:T(8,128)(2,1)}) %reduce-scatter.5.cloned.1.call-update) | async-done | bytes 589840 | tf_op jit(solution)/shard_map/reduce_scatter | solution.py:34
  803.7 7.5 all-to-all-start.3
  811.1 7.1 convolution_bitcast_fusion.1
  818.2 8.6 all-to-all-done.3
  826.8 1.4 reshape_reshape.7
  828.3 2.0 gather_fusion.1
  830.3 2.3 fusion.37
  833.7 76.0 %all-reduce.2 = (f32[1]{0:T(128)}, f32[1024]{0:T(1024)}) all-reduce(f32[1]{0:T(128)} %bitcast.51, f32[1024]{0:T(1024)S(1)} %get-tuple-element.6), channel_id=1, replica_groups=mesh['dp'=8,'expert'=32] {'dp','expert'}, use_global_device_ids=true, to_apply=%region_13.14 | all-reduce | flops 1025 | bytes 8200 | tf_op jit(solution)/shard_map/psum | solution.py:136
  909.8 121.4 %all-reduce.6.cloned.1.call-done = f32[1024,32]{0,1:T(8,128)} async-done(((f32[1024,32]{0,1:T(8,128)}), f32[1024,32]{0,1:T(8,128)}) %all-reduce.6.cloned.1.call-update) | async-done | bytes 131088 | tf_op jit(solution)/shard_map/psum | solution.py:136
  1031.1 1.6 copy.97
  (187 shorter events, 66.7 us)
Async XLA Ops:
  7.2 111.4 %copy-start = (bf16[1,1024,512]{2,1,0:T(8,128)(2,1)S(1)}, bf16[1,1024,512]{2,1,0:T(8,128)(2,1)}, u32[]{:S(2)}) copy-start(bf16[1,1024,512]{2,1,0:T(8,128)(2,1)} %param.14) | copy-start | bytes 3145732
  7.2 92.8 %all-gather.7.cloned.1.call-start = ((), (), s32[]{:S(2)}) async-start(), calls=%async_computation.9 | async-start | bytes 5308416 | tf_op jit(solution)/shard_map/all_gather | solution.py:27
  8.5 218.1 %copy-start.11 = (f32[212]{0:T(256)}, f32[212]{0:T(256)S(1)}, u32[]{:S(2)}) copy-start(f32[212]{0:T(256)S(1)} %broadcast_multiply_fusion.3) | copy-start | bytes 2548
  9.8 216.9 %copy-start.16 = (f32[212]{0:T(256)}, f32[212]{0:T(256)S(1)}, u32[]{:S(2)}) copy-start(f32[212]{0:T(256)S(1)} %add_rsqrt_fusion) | copy-start | bytes 2548
  12.8 127.0 %copy-start.25 = (s32[212,1]{0,1:T(1,128)}, s32[212,1]{0,1:T(1,128)S(1)}, u32[]{:S(2)}) copy-start(s32[212,1]{0,1:T(1,128)S(1)} %compare_select_fusion) | copy-start | bytes 2548
  39.4 158.6 %reduce-scatter.3.cloned.1.call-start = ((), (), s32[]{:S(2)}) async-start(), calls=%async_computation.6 | async-start | bytes 5308416 | tf_op jit(solution)/shard_map/reduce_scatter | solution.py:34
  118.6 16.3 %copy-start.28 = (bf16[1,512,1024]{2,1,0:T(8,128)(2,1)S(1)}, bf16[1,512,1024]{2,1,0:T(8,128)(2,1)}, u32[]{:S(2)}) copy-start(bf16[1,512,1024]{2,1,0:T(8,128)(2,1)} %param.15) | copy-start | bytes 3145732
  139.0 87.6 %copy-start.1 = (bf16[1,212,1024]{2,1,0:T(8,128)(2,1)S(1)}, bf16[1,212,1024]{2,1,0:T(8,128)(2,1)}, u32[]{:S(2)}) copy-start(bf16[1,212,1024]{2,1,0:T(8,128)(2,1)} %param.9) | copy-start | bytes 1302532
  139.0 87.6 %copy-start.9 = (f32[1024]{0:T(1024)S(1)}, f32[1024]{0:T(1024)}, u32[]{:S(2)}) copy-start(f32[1024]{0:T(1024)} %param.12) | copy-start | bytes 12292
  139.0 87.9 %copy-start.7 = (f32[1024,32]{0,1:T(8,128)S(1)}, f32[1024,32]{0,1:T(8,128)}, u32[]{:S(2)}) copy-start(f32[1024,32]{0,1:T(8,128)} %param.13) | copy-start | bytes 393220
  139.0 87.9 %copy-start.13 = (s32[1,212,1]{1,2,0:T(1,128)S(1)}, s32[1,212,1]{1,2,0:T(1,128)}, u32[]{:S(2)}) copy-start(s32[1,212,1]{1,2,0:T(1,128)} %param.10) | copy-start | bytes 2548
  139.8 103.9 %copy-start.26 = (f32[16]{0:T(128)}, f32[16]{0:T(128)S(1)}, u32[]{:S(2)}) copy-start(f32[16]{0:T(128)S(1)} %compare_convert_fusion) | copy-start | bytes 196
  139.8 102.6 %copy-start.18 = (s32[1024]{0:T(1024)}, s32[1024]{0:T(1024)S(1)}, u32[]{:S(2)}) copy-start(s32[1024]{0:T(1024)S(1)} %pad_clamp_fusion) | copy-start | bytes 12292
  219.1 23.0 %all-to-all-start.1 = ((bf16[32,1,1,9,1024]{4,3,2,1,0:T(8,128)(2,1)}), bf16[32,1,1,9,1024]{4,3,2,1,0:T(8,128)(2,1)S(1)}, u32[]{:S(2)}, u32[]{:S(2)}) async-start(bf16[32,1,1,9,1024]{4,3,2,1,0:T(8,128)(2,1)} %constant_dynamic-update-slice_fusion), calls=%async_computation.2 | async-start | bytes 2097152 | tf_op jit(solution)/shard_map/all_to_all | solution.py:43
  226.6 117.8 %all-gather.9.cloned.1.call-start = ((), (), s32[]{:S(2)}) async-start(), calls=%async_computation.10 | async-start | bytes 1052672 | tf_op jit(solution)/shard_map/all_gather | solution.py:102
  227.7 14.7 %copy-start.19 = (f32[212]{0:T(256)}, f32[212]{0:T(256)S(1)}, u32[]{:S(2)}) copy-start(f32[212]{0:T(256)S(1)} %fusion.16) | copy-start | bytes 2548
  227.7 15.8 %copy-start.21 = (f32[212]{0:T(256)}, f32[212]{0:T(256)S(1)}, u32[]{:S(2)}) copy-start(f32[212]{0:T(256)S(1)} %add_divide_fusion) | copy-start | bytes 2548
  245.7 359.4 %copy-start.8 = (f32[1024]{0:T(1024)S(1)}, f32[1024]{0:T(1024)}, u32[]{:S(2)}) copy-start(f32[1024]{0:T(1024)} %broadcast_divide_fusion) | copy-start | bytes 12292
  245.7 359.4 %all-reduce.8.cloned.1.call-start = ((), (), s32[]{:S(2)}) async-start(), calls=%async_computation.12 | async-start | bytes 2097152
  247.3 360.6 %copy-start.27 = (f32[16]{0:T(128)S(1)}, f32[16]{0:T(128)}, u32[]{:S(2)}) copy-start(f32[16]{0:T(128)} %copy-done.26) | copy-start | bytes 196
  247.4 360.7 %copy-start.22 = (f32[212]{0:T(256)S(1)}, f32[212]{0:T(256)}, u32[]{:S(2)}) copy-start(f32[212]{0:T(256)} %copy-done.21) | copy-start | bytes 2548
  348.5 344.0 %all-gather.11.cloned.1.call-start = ((), (), s32[]{:S(2)}) async-start(), calls=%async_computation.11 | async-start | bytes 5308416 | tf_op jit(solution)/shard_map/all_gather | solution.py:27
  635.4 147.6 %reduce-scatter.5.cloned.1.call-start = ((), (), s32[]{:S(2)}) async-start(), calls=%async_computation.7 | async-start | bytes 5308416 | tf_op jit(solution)/shard_map/reduce_scatter | solution.py:34
  701.2 9.9 copy-start.29
  724.0 307.2 %all-reduce.6.cloned.1.call-start = ((), (), s32[]{:S(2)}) async-start(), calls=%async_computation.8 | async-start | bytes 262144 | tf_op jit(solution)/shard_map/psum | solution.py:136
  725.2 8.0 copy-start.23
  803.7 23.1 %all-to-all-start.3 = ((bf16[32,1,1,9,1024]{4,3,2,1,0:T(8,128)(2,1)}), bf16[32,1,1,9,1024]{4,3,2,1,0:T(8,128)(2,1)}, u32[]{:S(2)}, u32[]{:S(2)}) async-start(bf16[32,1,1,9,1024]{4,3,2,1,0:T(8,128)(2,1)} %constant_dynamic-update-slice_fusion.32), calls=%async_computation.5 | async-start | bytes 2097152 | tf_op jit(solution)/shard_map/all_to_all | solution.py:43
  818.2 12.0 %copy-start.10 = (f32[1024]{0:T(1024)S(1)}, f32[1024]{0:T(1024)}, u32[]{:S(2)}) copy-start(f32[1024]{0:T(1024)} %param.12) | copy-start | bytes 12292
  818.2 12.0 %copy-start.12 = (f32[212]{0:T(256)S(1)}, f32[212]{0:T(256)}, u32[]{:S(2)}) copy-start(f32[212]{0:T(256)} %copy-done.11) | copy-start | bytes 2548
  818.2 12.0 %copy-start.15 = (s32[1,212,1]{1,2,0:T(1,128)S(1)}, s32[1,212,1]{1,2,0:T(1,128)}, u32[]{:S(2)}) copy-start(s32[1,212,1]{1,2,0:T(1,128)} %param.10) | copy-start | bytes 2548
  818.2 12.0 %copy-start.17 = (f32[212]{0:T(256)S(1)}, f32[212]{0:T(256)}, u32[]{:S(2)}) copy-start(f32[212]{0:T(256)} %copy-done.16) | copy-start | bytes 2548
  818.2 12.1 %copy-start.24 = (f32[212]{0:T(256)S(1)}, f32[212]{0:T(256)}, u32[]{:S(2)}) copy-start(f32[212]{0:T(256)} %copy-done.23) | copy-start | bytes 2548
  (8 other events, 13.5 us)
Sparse Core Ops, SparseCore 0:
  39.6 60.3 all-gather.6
  139.2 58.8 reduce-scatter.2
  245.8 98.4 all-gather.8
  350.2 254.8 all-reduce.7
  635.6 56.8 all-gather.10
  724.1 58.8 reduce-scatter.4
  790.0 241.1 all-reduce.5
